TPU v7x, 512 devices: a whole 4x4x16 slice. The times are simulated.
512 devices in a mesh: sec: 64 (over y, z), mpo: 8 (over x, core).
Axes of the slice: x: 4, y: 4, z: 16, core: 2. Of those that a mesh axis runs over, the one named last changes fastest.
Arguments:
- wavefunction: bfloat16 [64, 8, 512, 256], P('sec', None, 'mpo'), may hold values from -6 to 6
- left_env: bfloat16 [64, 40, 512, 512], P('sec', 'mpo'), may hold values from -0.0390625 to 0.0390625
- right_env: bfloat16 [64, 40, 256, 256], P('sec', 'mpo'), may hold values from -0.375 to 0.375
- left_dims: int32 [64], P('sec'), may hold values from 256 to 512
- right_dims: int32 [64], P('sec'), may hold values from 128 to 256
- term_shift: int32 [40], P('mpo'), may hold values from 0 to 4, as said below
Outputs:
- product: bfloat16 [64, 8, 512, 256], P('sec', None, 'mpo')
Inputs may be any that keep to these rules, and one draw needn't show every extreme that they name: `term_shift`: each of the five classes is named by exactly 8 terms.
All inputs are finite; a program needn't handle non-finite values.
Results may differ from a plain program's by a relative error of at most 0.0049.
Values may be sent and summed in bfloat16 or wider, within the bound.
A program may use at most 64 MiB of HBM per device.

v0:
```python
import jax
import jax.numpy as jnp
from jax import lax
from jax.sharding import PartitionSpec as P

SPINS = 8
number_steps = (0, 1, -1, 1, -1)
spin_steps = (0, 1, -1, -1, 1)


def shifted(array, axis, by):
    length = lax.axis_size(axis)
    pairs = [(i, i + by) for i in range(length) if 0 <= i + by < length]
    return lax.ppermute(array, axis, pairs)


def per_device(wavefunction, left_env, right_env, left_dims, right_dims, term_shift):
    row_share = wavefunction.shape[2]
    columns = wavefunction.shape[3]
    mpo_place = lax.axis_index("mpo")
    sector_id = lax.axis_index("sec")
    lattice_rows = lax.axis_size("sec") // SPINS
    rows_here = mpo_place * row_share + jnp.arange(row_share, dtype=jnp.int32)
    column_ids = jnp.arange(columns, dtype=jnp.int32)
    keep_mask = (rows_here[:, None] < left_dims[0]) & (column_ids[None, :] < right_dims[0])
    live_block = jnp.where(keep_mask[None, None], wavefunction, jnp.zeros_like(wavefunction))
    sector_line = sector_id // SPINS
    sector_place = sector_id % SPINS
    line_steps = jnp.array(number_steps, dtype=jnp.int32)
    place_steps = jnp.array(spin_steps, dtype=jnp.int32)
    source_line = sector_line - line_steps
    source_place = sector_place - place_steps
    inside = (
        (source_line >= 0)
        & (source_line < lattice_rows)
        & (source_place >= 0)
        & (source_place < SPINS)
    )
    selector = (
        (term_shift[:, None] == jnp.arange(5, dtype=jnp.int32)[None, :]) & inside[None, :]
    ).astype(jnp.bfloat16)
    full_block = lax.all_gather(live_block, "mpo", axis=2, tiled=True)
    neighbours = [full_block]
    for shift_class in range(1, 5):
        offset = number_steps[shift_class] * SPINS + spin_steps[shift_class]
        neighbours.append(shifted(full_block, "sec", offset))
    stacked = jnp.concatenate(neighbours, axis=0)
    selected = jnp.einsum(
        "tc,cvpq->tvpq", selector, stacked, preferred_element_type=jnp.float32
    ).astype(jnp.bfloat16)
    left_terms = left_env[0]
    right_terms = right_env[0]
    applied = jnp.einsum(
        "tpk,tvkq->tvpq", left_terms, selected, preferred_element_type=jnp.float32
    ).astype(jnp.bfloat16)
    term_total = jnp.einsum(
        "tvpk,tqk->vpq", applied, right_terms, preferred_element_type=jnp.float32
    )[None]
    row_sums = lax.psum_scatter(term_total, "mpo", scatter_dimension=2, tiled=True)
    return jnp.where(keep_mask[None, None], row_sums, jnp.zeros_like(row_sums)).astype(jnp.bfloat16)


def solution(mesh):
    in_specs = (
        P("sec", None, "mpo", None),
        P("sec", "mpo", None, None),
        P("sec", "mpo", None, None),
        P("sec"),
        P("sec"),
        P("mpo"),
    )
    out_specs = P("sec", None, "mpo", None)
    return jax.shard_map(
        per_device, mesh=mesh, in_specs=in_specs, out_specs=out_specs, check_vma=False
    )
```

profile of v0, /device:TPU:8, one launch (start us, length us, event | category | flops | bytes accessed | tf_op | source)
XLA Modules:
  0.0 792.9 jit_solution(16231609190747013689)
XLA Ops:
  6.5 0.0 copy-start
  6.5 0.0 all-gather.2.cloned.1.call-start
  8.0 0.1 broadcast_and_fusion
  8.1 1.7 broadcast_select_fusion
  9.8 0.0 all-gather.2.cloned.1.call-update
  9.8 0.0 reduce-scatter.2.cloned.1.call-start
  9.9 37.4 %all-gather.2.cloned.1.call-done = bf16[1,8,512,256]{3,2,1,0:T(8,128)(2,1)} async-done(((bf16[1,8,64,256]{3,2,1,0:T(8,128)(2,1)}), bf16[1,8,512,256]{3,2,1,0:T(8,128)(2,1)}) %all-gather.2.cloned.1.call-update) | async-done | bytes 2097168 | tf_op jit(solution)/shard_map/all_gather | solution.py:42
  47.3 12.0 %collective-permute-start = (bf16[1,8,512,256]{3,2,1,0:T(8,128)(2,1)}, bf16[1,8,512,256]{3,2,1,0:T(8,128)(2,1)}, u32[]{:S(2)}, u32[]{:S(2)}) collective-permute-start(bf16[1,8,512,256]{3,2,1,0:T(8,128)(2,1)} %all-gather.2.cloned.1.call-done), channel_id=1, source_target_pairs={{0,72},{8,80},{16,88},{24,96},{32,104},{40,112},{48,120},{56,128},... | collective-permute-start | bytes 6291464 | tf_op jit(solution)/shard_map/ppermute | solution.py:14
  59.3 2.7 collective-permute-start.1
  62.0 10.5 %collective-permute-start.2 = (bf16[1,8,512,256]{3,2,1,0:T(8,128)(2,1)}, bf16[1,8,512,256]{3,2,1,0:T(8,128)(2,1)}, u32[]{:S(2)}, u32[]{:S(2)}) collective-permute-start(bf16[1,8,512,256]{3,2,1,0:T(8,128)(2,1)} %all-gather.2.cloned.1.call-done), channel_id=1, source_target_pairs={{0,56},{8,64},{16,72},{24,80},{32,88},{40,96},{48,104},{56,112},{6... | collective-permute-start | bytes 6291464 | tf_op jit(solution)/shard_map/ppermute | solution.py:14
  72.5 4.0 collective-permute-start.3
  76.6 0.7 compare_and_fusion
  77.2 0.0 copy-start.1
  77.2 1.7 constant_dynamic-update-slice_fusion.4
  79.0 311.9 %collective-permute-done = bf16[1,8,512,256]{3,2,1,0:T(8,128)(2,1)} collective-permute-done((bf16[1,8,512,256]{3,2,1,0:T(8,128)(2,1)}, bf16[1,8,512,256]{3,2,1,0:T(8,128)(2,1)}, u32[]{:S(2)}, u32[]{:S(2)}) %collective-permute-start) | collective-permute-done | bytes 2097184 | tf_op jit(solution)/shard_map/ppermute | solution.py:14
  390.9 1.7 constant_dynamic-update-slice_fusion.3
  392.6 0.0 collective-permute-done.1
  392.7 1.7 constant_dynamic-update-slice_fusion.2
  394.4 296.8 %collective-permute-done.2 = bf16[1,8,512,256]{3,2,1,0:T(8,128)(2,1)} collective-permute-done((bf16[1,8,512,256]{3,2,1,0:T(8,128)(2,1)}, bf16[1,8,512,256]{3,2,1,0:T(8,128)(2,1)}, u32[]{:S(2)}, u32[]{:S(2)}) %collective-permute-start.2) | collective-permute-done | bytes 2097184 | tf_op jit(solution)/shard_map/ppermute | solution.py:14
  691.2 1.7 constant_dynamic-update-slice_fusion.1
  692.9 0.0 collective-permute-done.3
  692.9 1.7 constant_dynamic-update-slice_fusion
  694.7 0.0 copy-done.1
  694.7 0.0 copy-start.2
  694.7 24.2 %fusion = bf16[5,8,512,256]{3,0,2,1:T(8,128)(2,1)} fusion(bf16[5,8,512,256]{3,2,1,0:T(8,128)(2,1)S(1)} %constant_dynamic-update-slice_fusion, s32[5]{0:T(128)S(1)} %copy-done.1, pred[5]{0:T(512)(128)(4,1)S(1)} %compare_and_fusion), kind=kOutput, calls=%fused_computation.1 | convolution fusion | flops 52428848 | bytes 20971544 | tf_op jit(solution)/shard_map/tc,cvpq->tvpq/dot_general | solution.py:48
  718.9 0.0 copy-done
  718.9 0.0 copy-done.2
  718.9 16.6 %fusion.13 = f32[1,8,512,256]{3,2,1,0:T(8,128)} fusion(bf16[1,5,512,512]{3,2,1,0:T(8,128)(2,1)S(1)} %copy-done, bf16[1,5,256,256]{3,2,1,0:T(8,128)(2,1)S(1)} %copy-done.2, bf16[5,8,512,256]{3,0,2,1:T(8,128)(2,1)} %fusion), kind=kOutput, calls=%fused_computation.9 | convolution fusion | flops 8058306560 | bytes 17956864 | tf_op jit(solution)/shard_map/tvpk,tqk->vpq/dot_general | solution.py:56
  735.5 0.0 reduce-scatter.2.cloned.1.call-update
  735.5 48.7 %reduce-scatter.2.cloned.1.call-done = f32[1,8,64,256]{3,2,1,0:T(8,128)} async-done(((f32[1,8,512,256]{3,2,1,0:T(8,128)}), f32[1,8,64,256]{3,2,1,0:T(8,128)}) %reduce-scatter.2.cloned.1.call-update) | async-done | bytes 524304 | tf_op jit(solution)/shard_map/reduce_scatter | solution.py:59
  784.3 1.8 select_convert_fusion
  (2 shorter events, 0.0 us)
Async XLA Ops:
  6.5 712.4 %copy-start = (bf16[1,5,512,512]{3,2,1,0:T(8,128)(2,1)S(1)}, bf16[1,5,512,512]{3,2,1,0:T(8,128)(2,1)}, u32[]{:S(2)}) copy-start(bf16[1,5,512,512]{3,2,1,0:T(8,128)(2,1)} %param.9) | copy-start | bytes 7864324
  6.5 40.8 %all-gather.2.cloned.1.call-start = ((), (), s32[]{:S(2)}) async-start(), calls=%async_computation.1 | async-start | bytes 2359296 | tf_op jit(solution)/shard_map/all_gather | solution.py:42
  9.8 774.5 %reduce-scatter.2.cloned.1.call-start = ((), (), s32[]{:S(2)}) async-start(), calls=%async_computation.2 | async-start | bytes 4718592 | tf_op jit(solution)/shard_map/reduce_scatter | solution.py:59
  47.3 343.6 %collective-permute-start = (bf16[1,8,512,256]{3,2,1,0:T(8,128)(2,1)}, bf16[1,8,512,256]{3,2,1,0:T(8,128)(2,1)}, u32[]{:S(2)}, u32[]{:S(2)}) collective-permute-start(bf16[1,8,512,256]{3,2,1,0:T(8,128)(2,1)} %all-gather.2.cloned.1.call-done), channel_id=1, source_target_pairs={{0,72},{8,80},{16,88},{24,96},{32,104},{40,112},{48,120},{56,128},... | collective-permute-start | bytes 6291464 | tf_op jit(solution)/shard_map/ppermute | solution.py:14
  59.3 333.4 %collective-permute-start.1 = (bf16[1,8,512,256]{3,2,1,0:T(8,128)(2,1)}, bf16[1,8,512,256]{3,2,1,0:T(8,128)(2,1)}, u32[]{:S(2)}, u32[]{:S(2)}) collective-permute-start(bf16[1,8,512,256]{3,2,1,0:T(8,128)(2,1)} %all-gather.2.cloned.1.call-done), channel_id=1, source_target_pairs={{72,0},{80,8},{88,16},{96,24},{104,32},{112,40},{120,48},{128,56},... | collective-permute-start | bytes 6291464 | tf_op jit(solution)/shard_map/ppermute | solution.py:14
  62.0 629.2 %collective-permute-start.2 = (bf16[1,8,512,256]{3,2,1,0:T(8,128)(2,1)}, bf16[1,8,512,256]{3,2,1,0:T(8,128)(2,1)}, u32[]{:S(2)}, u32[]{:S(2)}) collective-permute-start(bf16[1,8,512,256]{3,2,1,0:T(8,128)(2,1)} %all-gather.2.cloned.1.call-done), channel_id=1, source_target_pairs={{0,56},{8,64},{16,72},{24,80},{32,88},{40,96},{48,104},{56,112},{6... | collective-permute-start | bytes 6291464 | tf_op jit(solution)/shard_map/ppermute | solution.py:14
  72.5 620.5 %collective-permute-start.3 = (bf16[1,8,512,256]{3,2,1,0:T(8,128)(2,1)}, bf16[1,8,512,256]{3,2,1,0:T(8,128)(2,1)}, u32[]{:S(2)}, u32[]{:S(2)}) collective-permute-start(bf16[1,8,512,256]{3,2,1,0:T(8,128)(2,1)} %all-gather.2.cloned.1.call-done), channel_id=1, source_target_pairs={{56,0},{64,8},{72,16},{80,24},{88,32},{96,40},{104,48},{112,56},{1... | collective-permute-start | bytes 6291464 | tf_op jit(solution)/shard_map/ppermute | solution.py:14
  77.2 617.4 %copy-start.1 = (s32[5]{0:T(128)S(1)}, s32[5]{0:T(128)}, u32[]{:S(2)}) copy-start(s32[5]{0:T(128)} %param.13) | copy-start | bytes 64
  694.7 24.2 %copy-start.2 = (bf16[1,5,256,256]{3,2,1,0:T(8,128)(2,1)S(1)}, bf16[1,5,256,256]{3,2,1,0:T(8,128)(2,1)}, u32[]{:S(2)}) copy-start(bf16[1,5,256,256]{3,2,1,0:T(8,128)(2,1)} %param.10) | copy-start | bytes 1966084
Sparse Core Ops, SparseCore 0:
  9.9 37.3 all-gather.1
  735.7 48.5 reduce-scatter.1
where the time goes:
time: 793 us
  waiting for transfers between devices  695 us (88%)
  matrix products  40.8 us (5%)
  starting transfers between devices  29.3 us (4%)
  between operations  15 us (2%)
  local copies, waits for them, and re-layouts  8.71 us (1%)
    ppermute x4, waiting for transfers between devices, shifted(): return lax.ppermute(array, axis, pairs)  609 us
    reduce_scatter x1, waiting for transfers between devices, per_device(): lax.psum_scatter(term_total, 'mpo', scatter_dimension=2, tiled=True)  48.7 us
    all_gather x1, waiting for transfers between devices, per_device(): full_block = lax.all_gather(live_block, 'mpo', axis=2, tiled=True)  37.4 us
    ppermute x4, starting transfers between devices, shifted(): return lax.ppermute(array, axis, pairs)  29.2 us
    dot_general x1, matrix products, per_device(): jnp.einsum('tc,cvpq->tvpq', selector, stacked, preferred_element_type=jnp...  24.2 us
    dot_general x1, matrix products, per_device(): jnp.einsum('tvpk,tqk->vpq', applied, right_terms, preferred_element_type=...  16.6 us
  transfers between devices with their start and end apart: 6, of which 4 were waited for; matrix products, arithmetic and copies ran while one was open for 1% of the time, Pallas kernels for 0%

commit v1 on v0

--- a/solution.py
+++ b/solution.py
@@ -39,7 +39,9 @@
     selector = (
         (term_shift[:, None] == jnp.arange(5, dtype=jnp.int32)[None, :]) & inside[None, :]
     ).astype(jnp.bfloat16)
-    full_block = lax.all_gather(live_block, "mpo", axis=2, tiled=True)
+    full_block = jnp.concatenate(
+        lax.all_to_all(jnp.stack([live_block] * lax.axis_size("mpo")), "mpo", 0, 0), axis=2
+    )
     neighbours = [full_block]
     for shift_class in range(1, 5):
         offset = number_steps[shift_class] * SPINS + spin_steps[shift_class]

time: 793 us -> 877 us (1.11); the launches traced: 793 us -> 868 us
  local copies, waits for them, and re-layouts: 8.71 us -> 112 us
  waiting for transfers between devices: 695 us -> 642 us
  blocking collectives: 0 us -> 31.3 us
    concatenate x1, local copies, waits for them, and re-layouts: 1.74 us -> 74.4 us  [per_device(): stacked = jnp.concatenate(neighbours, axis=0)]
    all_gather x1 -> x0, waiting for transfers between devices: 37.4 us -> none  [per_device(): full_block = lax.all_gather(live_block, 'mpo', axis=2, tiled=True)]
    all_to_all x0 -> x1, blocking collectives: none -> 31.3 us  [per_device(): lax.all_to_all(jnp.stack([live_block] * lax.axis_size('mpo')), 'mpo', 0, 0)]
    ppermute x0 -> x4, local copies, waits for them, and re-layouts: none -> 28.5 us  [shifted(): return lax.ppermute(array, axis, pairs)]
    dot_general x1, matrix products: 24.2 us -> 14.9 us  [per_device(): jnp.einsum('tc,cvpq->tvpq', selector, stacked, preferred_element_type=jnp...]
  transfers between devices with their start and end apart: 6 -> 5, of which waited for: 4 -> 4; matrix products, arithmetic and copies ran while one was open for 1% -> 3% of each run, Pallas kernels for 0% -> 0%
where the time goes in v1:
time: 877 us; the launch traced here: 868 us
  waiting for transfers between devices  642 us (73%)
  local copies, waits for them, and re-layouts  112 us (13%)
  matrix products  33.1 us (4%)
  starting transfers between devices  31.7 us (4%)
  blocking collectives  31.3 us (4%)
  between operations  15 us (2%)
    ppermute x4, waiting for transfers between devices, shifted(): return lax.ppermute(array, axis, pairs)  601 us
    concatenate x1, local copies, waits for them, and re-layouts, per_device(): stacked = jnp.concatenate(neighbours, axis=0)  74.4 us
    reduce_scatter x1, waiting for transfers between devices, per_device(): lax.psum_scatter(term_total, 'mpo', scatter_dimension=2, tiled=True)  41.2 us
    ppermute x4, starting transfers between devices, shifted(): return lax.ppermute(array, axis, pairs)  31.7 us
    all_to_all x1, blocking collectives, per_device(): lax.all_to_all(jnp.stack([live_block] * lax.axis_size('mpo')), 'mpo', 0, 0)  31.3 us
    ppermute x4, local copies, waits for them, and re-layouts, shifted(): return lax.ppermute(array, axis, pairs)  28.5 us
    dot_general x1, matrix products, per_device(): jnp.einsum('tvpk,tqk->vpq', applied, right_terms, preferred_element_type=...  18.2 us
  transfers between devices with their start and end apart: 5, of which 4 were waited for; matrix products, arithmetic and copies ran while one was open for 3% of the time, Pallas kernels for 0%

profile of v1, /device:TPU:8, one launch (start us, length us, event | category | flops | bytes accessed | tf_op | source)
XLA Modules:
  0.0 867.5 jit_solution(4606943991521428210)
XLA Ops:
  6.5 0.0 copy-start
  6.5 0.0 reduce-scatter.2.cloned.1.call-start
  8.0 0.1 broadcast_and_fusion
  8.1 1.0 select_bitcast_fusion
  9.1 0.2 stack.2
  9.3 0.0 copy-start.2
  9.3 0.0 copy-start.3
  9.4 31.3 %all_to_all.5 = bf16[8,1,8,64,256]{4,3,2,1,0:T(8,128)(2,1)S(1)} all-to-all(bf16[8,1,8,64,256]{4,3,2,1,0:T(8,128)(2,1)S(1)} %stack.2), channel_id=1, replica_groups=mesh['sec'=64,'mpo'=8] {'mpo'}, dimensions={0} | all-to-all | bytes 4194304 | tf_op jit(solution)/shard_map/all_to_all | solution.py:43
  40.7 1.5 copy.17
  42.1 15.2 %collective-permute-start.3 = (bf16[1,8,512,256]{3,2,1,0:T(8,128)(2,1)}, bf16[1,8,512,256]{3,2,1,0:T(8,128)(2,1)}, u32[]{:S(2)}, u32[]{:S(2)}) collective-permute-start(bf16[1,8,512,256]{3,2,1,0:T(8,128)(2,1)} %bitcast.6), channel_id=1, source_target_pairs={{56,0},{64,8},{72,16},{80,24},{88,32},{96,40},{104,48},{112,56},{1... | collective-permute-start | bytes 6291464 | tf_op jit(solution)/shard_map/ppermute | solution.py:14
  57.3 1.9 collective-permute-start.2
  59.2 9.6 %collective-permute-start.1 = (bf16[1,8,512,256]{3,2,1,0:T(8,128)(2,1)}, bf16[1,8,512,256]{3,2,1,0:T(8,128)(2,1)}, u32[]{:S(2)}, u32[]{:S(2)}) collective-permute-start(bf16[1,8,512,256]{3,2,1,0:T(8,128)(2,1)} %bitcast.6), channel_id=1, source_target_pairs={{72,0},{80,8},{88,16},{96,24},{104,32},{112,40},{120,48},{128,56},... | collective-permute-start | bytes 6291464 | tf_op jit(solution)/shard_map/ppermute | solution.py:14
  68.9 5.1 collective-permute-start
  73.9 0.0 copy-done.2
  74.0 0.0 copy-done.3
  74.0 7.0 copy.18
  81.0 293.1 %collective-permute-done.3 = bf16[1,8,512,256]{3,2,1,0:T(8,128)(2,1)} collective-permute-done((bf16[1,8,512,256]{3,2,1,0:T(8,128)(2,1)}, bf16[1,8,512,256]{3,2,1,0:T(8,128)(2,1)}, u32[]{:S(2)}, u32[]{:S(2)}) %collective-permute-start.3) | collective-permute-done | bytes 2097184 | tf_op jit(solution)/shard_map/ppermute | solution.py:14
  374.1 7.1 copy.22
  381.2 7.1 collective-permute-done.2
  388.3 7.1 copy.21
  395.3 300.6 %collective-permute-done.1 = bf16[1,8,512,256]{3,2,1,0:T(8,128)(2,1)} collective-permute-done((bf16[1,8,512,256]{3,2,1,0:T(8,128)(2,1)}, bf16[1,8,512,256]{3,2,1,0:T(8,128)(2,1)}, u32[]{:S(2)}, u32[]{:S(2)}) %collective-permute-start.1) | collective-permute-done | bytes 2097184 | tf_op jit(solution)/shard_map/ppermute | solution.py:14
  695.9 7.2 copy.20
  703.1 0.0 collective-permute-done
  703.1 7.2 copy.19
  710.3 74.4 %concatenate.3 = bf16[5,8,512,256]{3,0,2,1:T(8,128)(2,1)} concatenate(bf16[1,8,512,256]{3,0,2,1:T(2,128)(2,1)} %copy.18, bf16[1,8,512,256]{3,0,2,1:T(2,128)(2,1)} %copy.19, bf16[1,8,512,256]{3,0,2,1:T(2,128)(2,1)} %copy.20, bf16[1,8,512,256]{3,0,2,1:T(2,128)(2,1)} %copy.21, bf16[1,8,512,256]{3,0,2,1:T(2,128)(2,1)} %copy.22), dimensions={0} | concatenate | bytes 20971520 | tf_op jit(solution)/shard_map/concatenate | solution.py:49
  784.7 0.0 copy-done.1
  784.7 14.9 %convolution_convert_fusion = bf16[5,8,512,256]{3,0,2,1:T(8,128)(2,1)} fusion(bf16[5,8,512,256]{3,0,2,1:T(8,128)(2,1)} %concatenate.3, s32[5]{0:T(128)S(1)} %copy-done.1, pred[5]{0:T(512)(128)(4,1)S(1)} %compare_and_fusion), kind=kOutput, calls=%fused_computation.5 | convolution fusion | flops 57671728 | bytes 20971544 | tf_op jit(solution)/shard_map/tc,cvpq->tvpq/dot_general | solution.py:50
  799.5 0.0 copy-done
  799.5 18.2 %fusion.11 = f32[1,8,512,256]{3,2,1,0:T(8,128)} fusion(bf16[5,8,512,256]{3,0,2,1:T(8,128)(2,1)} %convolution_convert_fusion, bf16[1,5,512,512]{3,2,1,0:T(8,128)(2,1)S(1)} %copy-done, bf16[1,5,256,256]{3,2,1,0:T(8,128)(2,1)S(1)} %copy-done.4), kind=kOutput, calls=%fused_computation.7 | convolution fusion | flops 8058306560 | bytes 17956864 | tf_op jit(solution)/shard_map/tvpk,tqk->vpq/dot_general | solution.py:58
  817.7 0.0 reduce-scatter.2.cloned.1.call-update
  817.7 41.2 %reduce-scatter.2.cloned.1.call-done = f32[1,8,64,256]{3,2,1,0:T(8,128)} async-done(((f32[1,8,512,256]{3,2,1,0:T(8,128)}), f32[1,8,64,256]{3,2,1,0:T(8,128)}) %reduce-scatter.2.cloned.1.call-update) | async-done | bytes 524304 | tf_op jit(solution)/shard_map/reduce_scatter | solution.py:61
  858.9 1.8 select_convert_fusion
  (6 shorter events, 0.0 us)
Async XLA Ops:
  6.5 793.0 %copy-start = (bf16[1,5,512,512]{3,2,1,0:T(8,128)(2,1)S(1)}, bf16[1,5,512,512]{3,2,1,0:T(8,128)(2,1)}, u32[]{:S(2)}) copy-start(bf16[1,5,512,512]{3,2,1,0:T(8,128)(2,1)} %param.9) | copy-start | bytes 7864324
  6.5 852.4 %reduce-scatter.2.cloned.1.call-start = ((), (), s32[]{:S(2)}) async-start(), calls=%async_computation.2 | async-start | bytes 4718592 | tf_op jit(solution)/shard_map/reduce_scatter | solution.py:61
  9.3 64.6 %copy-start.2 = (s32[5]{0:T(128)S(1)}, s32[5]{0:T(128)}, u32[]{:S(2)}) copy-start(s32[5]{0:T(128)} %constant.56) | copy-start | bytes 64
  9.3 64.6 %copy-start.3 = (s32[5]{0:T(128)S(1)}, s32[5]{0:T(128)}, u32[]{:S(2)}) copy-start(s32[5]{0:T(128)} %constant.55) | copy-start | bytes 64
  42.1 332.0 %collective-permute-start.3 = (bf16[1,8,512,256]{3,2,1,0:T(8,128)(2,1)}, bf16[1,8,512,256]{3,2,1,0:T(8,128)(2,1)}, u32[]{:S(2)}, u32[]{:S(2)}) collective-permute-start(bf16[1,8,512,256]{3,2,1,0:T(8,128)(2,1)} %bitcast.6), channel_id=1, source_target_pairs={{56,0},{64,8},{72,16},{80,24},{88,32},{96,40},{104,48},{112,56},{1... | collective-permute-start | bytes 6291464 | tf_op jit(solution)/shard_map/ppermute | solution.py:14
  57.3 331.0 %collective-permute-start.2 = (bf16[1,8,512,256]{3,2,1,0:T(8,128)(2,1)}, bf16[1,8,512,256]{3,2,1,0:T(8,128)(2,1)}, u32[]{:S(2)}, u32[]{:S(2)}) collective-permute-start(bf16[1,8,512,256]{3,2,1,0:T(8,128)(2,1)} %bitcast.6), channel_id=1, source_target_pairs={{0,56},{8,64},{16,72},{24,80},{32,88},{40,96},{48,104},{56,112},{6... | collective-permute-start | bytes 6291464 | tf_op jit(solution)/shard_map/ppermute | solution.py:14
  59.2 636.7 %collective-permute-start.1 = (bf16[1,8,512,256]{3,2,1,0:T(8,128)(2,1)}, bf16[1,8,512,256]{3,2,1,0:T(8,128)(2,1)}, u32[]{:S(2)}, u32[]{:S(2)}) collective-permute-start(bf16[1,8,512,256]{3,2,1,0:T(8,128)(2,1)} %bitcast.6), channel_id=1, source_target_pairs={{72,0},{80,8},{88,16},{96,24},{104,32},{112,40},{120,48},{128,56},... | collective-permute-start | bytes 6291464 | tf_op jit(solution)/shard_map/ppermute | solution.py:14
  68.9 634.2 %collective-permute-start = (bf16[1,8,512,256]{3,2,1,0:T(8,128)(2,1)}, bf16[1,8,512,256]{3,2,1,0:T(8,128)(2,1)}, u32[]{:S(2)}, u32[]{:S(2)}) collective-permute-start(bf16[1,8,512,256]{3,2,1,0:T(8,128)(2,1)} %bitcast.6), channel_id=1, source_target_pairs={{0,72},{8,80},{16,88},{24,96},{32,104},{40,112},{48,120},{56,128},... | collective-permute-start | bytes 6291464 | tf_op jit(solution)/shard_map/ppermute | solution.py:14
  710.3 74.4 %copy-start.1 = (s32[5]{0:T(128)S(1)}, s32[5]{0:T(128)}, u32[]{:S(2)}) copy-start(s32[5]{0:T(128)} %param.13) | copy-start | bytes 64
  784.7 14.9 %copy-start.4 = (bf16[1,5,256,256]{3,2,1,0:T(8,128)(2,1)S(1)}, bf16[1,5,256,256]{3,2,1,0:T(8,128)(2,1)}, u32[]{:S(2)}) copy-start(bf16[1,5,256,256]{3,2,1,0:T(8,128)(2,1)} %param.10) | copy-start | bytes 1966084
Sparse Core Ops, SparseCore 0:
  817.9 40.9 reduce-scatter.1
